TPU v7x, 256 devices: a whole 4x4x8 slice. The times are simulated.
256 devices in a mesh: row: 8 (over z), col: 4 (over x_hi, core), chan: 8 (over x_lo, y).
Axes of the slice: x: 4 (x_hi: 2, x_lo: 2; x = x_hi * 2 + x_lo), y: 4, z: 8, core: 2. Of those that a mesh axis runs over, the one named last changes fastest.
Arguments:
- alignment_features: bfloat16 [2048, 512, 64], P('col', 'row'), may hold values from -8 to 8
- alignment_row_mask: int32 [2048], P('col'), may hold values 0 or 1
- residue_token_mask: int32 [512], P('row'), may hold values 0 or 1
- layer_norm_gain: float32 [64], replicated, may hold values from 0.25 to 1.75
- layer_norm_bias: float32 [64], replicated, may hold values from -3 to 3
- left_factor_weight: bfloat16 [64, 32], P(None, 'chan'), may hold values from -0.75 to 0.75
- right_factor_weight: bfloat16 [64, 32], replicated, may hold values from -0.75 to 0.75
- output_weight: bfloat16 [1024, 128], P('chan'), may hold values from -0.1875 to 0.1875
- output_bias: float32 [128], replicated, may hold values from -3 to 3
Outputs:
- pair_update: bfloat16 [512, 512, 128], P('col', ('row', 'chan'))
All inputs are finite; a program needn't handle non-finite values. No bound on the sum of `alignment_row_mask` or of `residue_token_mask` on one device may be relied on, other than what follows from the above.
Results may differ from a plain program's by a relative error of at most 0.0038.
Values may be sent and summed in bfloat16 or wider, within the bound.
No kernel may reach another device: no remote copies, remote signals or barrier semaphores. Data moves between devices by JAX's collectives and lax.ppermute only.
A program may use at most 128 MiB of HBM per device.

v0:
```python
import jax
import jax.numpy as jnp
from jax import lax
from jax.sharding import PartitionSpec as P


def apply_layer_norm(features, layer_norm_gain, layer_norm_bias):
    values = features.astype(jnp.float32)
    center = values - jnp.mean(values, axis=-1, keepdims=True)
    spread = jnp.mean(center * center, axis=-1, keepdims=True)
    return (center * lax.rsqrt(spread + 1e-05) * layer_norm_gain + layer_norm_bias).astype(
        jnp.bfloat16
    )


def make_factors(
    features,
    rows_used,
    tokens_used,
    layer_norm_gain,
    layer_norm_bias,
    left_factor_weight,
    right_factor_weight,
):
    normalized_features = apply_layer_norm(features, layer_norm_gain, layer_norm_bias)
    weight = rows_used[:, None].astype(jnp.float32) * tokens_used[None, :].astype(jnp.float32)
    left_part = (
        jnp.einsum(
            "stm,mc->sct",
            normalized_features,
            left_factor_weight,
            preferred_element_type=jnp.float32,
        )
        * weight[:, None, :]
    )
    right_part = (
        jnp.einsum(
            "stm,me->ste",
            normalized_features,
            right_factor_weight,
            preferred_element_type=jnp.float32,
        )
        * weight[:, :, None]
    )
    return (left_part.astype(jnp.bfloat16), right_part.astype(jnp.bfloat16))


def body(
    alignment_features,
    alignment_row_mask,
    residue_token_mask,
    layer_norm_gain,
    layer_norm_bias,
    left_factor_weight,
    right_factor_weight,
    output_weight,
    output_bias,
):
    every_feature, every_row = (
        lax.all_gather(alignment_features, "col", axis=0, tiled=True),
        lax.all_gather(alignment_row_mask, "col", axis=0, tiled=True),
    )
    left_part, right_every = make_factors(
        every_feature,
        every_row,
        residue_token_mask,
        layer_norm_gain,
        layer_norm_bias,
        left_factor_weight,
        right_factor_weight,
    )
    tokens_here = residue_token_mask.shape[0]
    mask_shaped = residue_token_mask.reshape(1, 1, tokens_here)
    owner_count = lax.axis_size("row") // lax.axis_size("col")
    block_tokens = tokens_here * owner_count
    col_index = lax.axis_index("col")
    left_every, mask_every = (
        lax.all_gather(left_part, "row", axis=2, tiled=True),
        lax.all_gather(mask_shaped, "row", axis=2, tiled=True),
    )
    left_block = lax.dynamic_slice_in_dim(left_every, col_index * block_tokens, block_tokens, 2)
    mask_block = lax.dynamic_slice_in_dim(mask_every, col_index * block_tokens, block_tokens, 2)
    products = jnp.einsum(
        "sci,sje->ijce", left_block, right_every, preferred_element_type=jnp.float32
    ).astype(jnp.bfloat16)
    flat_products = products.reshape(block_tokens * tokens_here, -1)
    partial_pairs = jnp.dot(
        flat_products, output_weight, preferred_element_type=jnp.float32
    ).reshape(block_tokens, tokens_here, -1)
    chan_count = lax.axis_size("chan")
    share = tokens_here // chan_count
    chan_index = lax.axis_index("chan")
    total_pairs = lax.psum(partial_pairs, "chan")
    summed = lax.dynamic_slice_in_dim(total_pairs, chan_index * share, share, 1)
    row_total = jnp.sum(every_row).astype(jnp.float32)
    first_used = mask_block.reshape(block_tokens).astype(jnp.float32)
    second_used = lax.dynamic_slice_in_dim(residue_token_mask, chan_index * share, share, 0).astype(
        jnp.float32
    )
    count = jnp.maximum(row_total * first_used[:, None] * second_used[None, :], 1.0)
    return ((summed + output_bias) / count[:, :, None]).astype(jnp.bfloat16)


def solution(mesh):
    in_specs = (
        P("col", "row", None),
        P("col"),
        P("row"),
        P(),
        P(),
        P(None, "chan"),
        P(),
        P("chan", None),
        P(),
    )
    out_specs = P("col", ("row", "chan"), None)
    return jax.shard_map(body, mesh=mesh, in_specs=in_specs, out_specs=out_specs, check_vma=False)
```

profile of v0, /device:TPU:1, one launch (start us, length us, event | category | flops | bytes accessed | tf_op | source)
XLA Modules:
  0.0 390.0 jit_solution(13971857495411139468)
XLA Ops:
  6.5 0.0 copy-start
  6.5 0.0 all-gather.5.cloned.1.call-start
  6.5 0.7 all-gather.5.cloned.1.call-update
  7.3 0.0 all-gather.7.cloned.1.call-start
  7.3 0.7 convert_element_type.49
  8.0 9.9 %all-gather.1 = s32[4,1,512]{2,1,0:T(1,128)S(1)} all-gather(s32[1,1,512]{2,1,0:T(1,128)} %bitcast.35), channel_id=1, replica_groups=mesh['row'=8,'col'=4,'chan'=8] {'col'}, dimensions={0}, use_global_device_ids=true | all-gather | bytes 10240 | tf_op jit(solution)/shard_map/all_gather | solution.py:61
  17.8 0.6 fusion.25
  18.5 0.1 broadcast_multiply_fusion
  18.6 0.0 copy-start.4
  18.6 0.0 copy-start.5
  18.6 107.3 %all-gather.5.cloned.1.call-done = bf16[2048,64,64]{0,2,1:T(8,128)(2,1)} async-done(((bf16[512,64,64]{0,2,1:T(8,128)(2,1)}), bf16[2048,64,64]{0,2,1:T(8,128)(2,1)}) %all-gather.5.cloned.1.call-update) | async-done | bytes 16777232 | tf_op jit(solution)/shard_map/all_gather | solution.py:60
  125.9 0.0 copy-start.1
  125.9 7.4 %convert_reduce_fusion = f32[2048,64]{0,1:T(8,128)S(1)} fusion(bf16[2048,64,64]{0,2,1:T(8,128)(2,1)} %all-gather.5.cloned.1.call-done), kind=kLoop, calls=%fused_computation.1 | loop fusion | flops 16646144 | bytes 17301504 | tf_op jit(solution)/shard_map/reduce_sum | solution.py:9
  133.3 3.2 copy-done.1
  136.5 5.4 %fusion.2 = f32[2048,64]{0,1:T(8,128)S(1)} fusion(bf16[2048,64,64]{0,2,1:T(8,128)(2,1)S(1)} %copy-done.1, f32[2048,64]{0,1:T(8,128)S(1)} %broadcast_multiply_fusion.1), kind=kLoop, calls=%fused_computation.4 | loop fusion | flops 33423360 | bytes 17825792 | tf_op jit(solution)/shard_map/reduce_sum | solution.py:10
  141.9 0.1 add_rsqrt_fusion
  142.0 0.0 copy-done.4
  142.0 0.0 copy-done.5
  142.0 0.0 copy-start.3
  142.0 6.6 %fusion.5 = bf16[2048,64,64]{0,2,1:T(8,128)(2,1)S(1)} fusion(bf16[2048,64,64]{0,2,1:T(8,128)(2,1)S(1)} %copy-done.1, f32[64]{0:T(128)S(1)} %copy-done.4, f32[64]{0:T(128)S(1)} %copy-done.5, f32[2048,64]{0,1:T(8,128)S(1)} %add_rsqrt_fusion, f32[2048,64]{0,1:T(8,128)S(1)} %broadcast_multiply_fusion.1), kind=kLoop, calls=%fused_computation.7 | loop fusion | flops 50331648 | bytes 34603520 | tf_op jit(solution)/shard_map/convert_element_type | solution.py:11
  148.7 0.0 copy-start.2
  148.7 5.7 %copy-done.2 = bf16[2048,64,64]{0,2,1:T(8,128)(2,1)} copy-done((bf16[2048,64,64]{0,2,1:T(8,128)(2,1)}, bf16[2048,64,64]{0,2,1:T(8,128)(2,1)S(1)}, u32[]{:S(2)}) %copy-start.2) | copy-done | bytes 16777240
  154.4 0.0 copy-done.3
  154.4 0.0 copy-start.7
  154.4 5.2 %fusion.13 = bf16[2048,4,64]{0,1,2:T(4,128)(2,1)} fusion(bf16[2048,64,64]{0,2,1:T(8,128)(2,1)S(1)} %fusion.5, f32[2048,64]{0,1:T(8,128)S(1)} %broadcast_multiply_fusion, bf16[64,4]{0,1:T(4,128)(2,1)S(1)} %copy-done.3), kind=kOutput, calls=%fused_computation.15 | convolution fusion | flops 68157440 | bytes 18350592 | tf_op jit(solution)/shard_map/stm,mc->sct/dot_general | solution.py:28
  159.6 0.0 all-gather.7.cloned.1.call-update
  159.6 0.0 all-reduce.3.cloned.1.call-start
  159.7 93.1 %all-gather.7.cloned.1.call-done = bf16[2048,4,512]{0,1,2:T(4,128)(2,1)} async-done(((bf16[2048,4,64]{0,1,2:T(4,128)(2,1)}), bf16[2048,4,512]{0,1,2:T(4,128)(2,1)}) %all-gather.7.cloned.1.call-update) | async-done | bytes 8388624 | tf_op jit(solution)/shard_map/all_gather | solution.py:78
  252.7 2.6 constant_dynamic-slice_fusion
  255.3 3.0 copy.18
  258.4 0.0 copy-done.7
  258.4 0.0 copy-start.9
  258.4 0.0 copy-start.8
  258.4 0.0 copy-start.6
  258.4 11.0 %fusion.15 = bf16[64,32,4,128]{3,1,2,0:T(8,128)(2,1)S(1)} fusion(bf16[2048,4,128]{2,0,1:T(8,128)(2,1)} %copy.18, f32[2048,64]{0,1:T(8,128)S(1)} %broadcast_multiply_fusion, bf16[2048,64,64]{0,2,1:T(8,128)(2,1)} %copy-done.2, bf16[64,32]{0,1:T(8,128)(2,1)S(1)} %copy-done.7), kind=kOutput, calls=%fused_computation.17 | convolution fusion | flops 4841275392 | bytes 21499904 | tf_op jit(solution)/shard_map/sci,sje->ijce/dot_general | solution.py:83
  269.4 0.0 copy-done
  269.4 2.7 fusion.20
  272.2 0.0 all-reduce.3.cloned.1.call-update
  272.8 0.0 copy-done.9
  272.9 0.6 dynamic-slice.1
  274.1 0.0 copy-done.8
  274.1 0.2 dynamic-update-slice
  274.4 9.1 %all-reduce = s32[512]{0:T(512)S(1)} all-reduce(s32[512]{0:T(512)S(1)} %dynamic-update-slice), channel_id=2, replica_groups=mesh['row'=8,'col'=4,'chan'=8] {'row'}, use_global_device_ids=true, to_apply=%add | all-reduce | flops 512 | bytes 4096
  283.5 0.1 dynamic-slice_convert_fusion
  283.5 0.1 convert_multiply_fusion
  283.6 0.1 multiply_maximum_fusion
  283.7 97.7 %all-reduce.3.cloned.1.call-done = f32[128,64,128]{2,0,1:T(8,128)} async-done(((f32[128,64,128]{2,0,1:T(8,128)}), f32[128,64,128]{2,0,1:T(8,128)}) %all-reduce.3.cloned.1.call-update) | async-done | bytes 4194320 | tf_op jit(solution)/shard_map/psum | solution.py:93
  381.3 0.0 copy-done.6
  381.3 1.2 divide_convert_fusion
  382.6 0.9 copy.15
  (2 shorter events, 0.0 us)
Async XLA Ops:
  6.5 262.9 %copy-start = (bf16[128,128]{1,0:T(8,128)(2,1)S(1)}, bf16[128,128]{1,0:T(8,128)(2,1)}, u32[]{:S(2)}) copy-start(bf16[128,128]{1,0:T(8,128)(2,1)} %param.16) | copy-start | bytes 98308
  6.5 119.3 %all-gather.5.cloned.1.call-start = ((), (), s32[]{:S(2)}) async-start(), calls=%async_computation | async-start | bytes 20971520 | tf_op jit(solution)/shard_map/all_gather | solution.py:60
  7.3 245.5 %all-gather.7.cloned.1.call-start = ((), (), s32[]{:S(2)}) async-start(), calls=%async_computation.1 | async-start | bytes 9437184 | tf_op jit(solution)/shard_map/all_gather | solution.py:78
  18.6 123.4 %copy-start.4 = (f32[64]{0:T(128)S(1)}, f32[64]{0:T(128)}, u32[]{:S(2)}) copy-start(f32[64]{0:T(128)} %param.13) | copy-start | bytes 772
  18.6 123.4 %copy-start.5 = (f32[64]{0:T(128)S(1)}, f32[64]{0:T(128)}, u32[]{:S(2)}) copy-start(f32[64]{0:T(128)} %param.12) | copy-start | bytes 772
  125.9 10.7 %copy-start.1 = (bf16[2048,64,64]{0,2,1:T(8,128)(2,1)S(1)}, bf16[2048,64,64]{0,2,1:T(8,128)(2,1)}, u32[]{:S(2)}) copy-start(bf16[2048,64,64]{0,2,1:T(8,128)(2,1)} %all-gather.5.cloned.1.call-done) | copy-start | bytes 50331652
  142.0 12.4 %copy-start.3 = (bf16[64,4]{0,1:T(4,128)(2,1)S(1)}, bf16[64,4]{0,1:T(4,128)(2,1)}, u32[]{:S(2)}) copy-start(bf16[64,4]{0,1:T(4,128)(2,1)} %param.14) | copy-start | bytes 1540
  148.7 5.7 %copy-start.2 = (bf16[2048,64,64]{0,2,1:T(8,128)(2,1)}, bf16[2048,64,64]{0,2,1:T(8,128)(2,1)S(1)}, u32[]{:S(2)}) copy-start(bf16[2048,64,64]{0,2,1:T(8,128)(2,1)S(1)} %fusion.5) | copy-start | bytes 50331652
  154.4 104.0 %copy-start.7 = (bf16[64,32]{0,1:T(8,128)(2,1)S(1)}, bf16[64,32]{0,1:T(8,128)(2,1)}, u32[]{:S(2)}) copy-start(bf16[64,32]{0,1:T(8,128)(2,1)} %param.15) | copy-start | bytes 12292
  159.6 221.7 %all-reduce.3.cloned.1.call-start = ((), (), s32[]{:S(2)}) async-start(), calls=%async_computation.2 | async-start | bytes 8388608 | tf_op jit(solution)/shard_map/psum | solution.py:93
  258.4 14.5 %copy-start.9 = (u32[256]{0:T(256)S(1)}, u32[256]{0:T(256)}, u32[]{:S(2)}) copy-start(u32[256]{0:T(256)} %constant.32) | copy-start | bytes 3076
  258.4 15.7 %copy-start.8 = (s32[64]{0:T(128)S(1)}, s32[64]{0:T(128)}, u32[]{:S(2)}) copy-start(s32[64]{0:T(128)} %param.11) | copy-start | bytes 772
  258.4 123.0 %copy-start.6 = (f32[128]{0:T(128)S(1)}, f32[128]{0:T(128)}, u32[]{:S(2)}) copy-start(f32[128]{0:T(128)} %param.17) | copy-start | bytes 1540
Sparse Core Ops, SparseCore 0:
  9.1 116.6 all-gather.4
  159.7 92.9 all-gather.6
  272.3 108.9 all-reduce.2
where the time goes:
time: 390 us
  waiting for transfers between devices  299 us (77%)
  other arithmetic  22.4 us (6%)
  blocking collectives  19 us (5%)
  matrix products  19 us (5%)
  local copies, waits for them, and re-layouts  16.3 us (4%)
  between operations  14.6 us (4%)
    all_gather x1, waiting for transfers between devices, body(): lax.all_gather(alignment_features, 'col', axis=0, tiled=True)  107 us
    psum x1, waiting for transfers between devices, body(): total_pairs = lax.psum(partial_pairs, 'chan')  97.7 us
    all_gather x1, waiting for transfers between devices, body(): lax.all_gather(left_part, 'row', axis=2, tiled=True)  93.1 us
    unnamed x24, local copies, waits for them, and re-layouts  12.8 us
    dot_general x1, matrix products, body(): jnp.einsum('sci,sje->ijce', left_block, right_every, preferred_element_ty...  11 us
    all_gather x1, blocking collectives, body(): lax.all_gather(alignment_row_mask, 'col', axis=0, tiled=True)  9.85 us
    unnamed x1, blocking collectives  9.1 us
  transfers between devices with their start and end apart: 3, of which 3 were waited for; matrix products, arithmetic and copies ran while one was open for 1% of the time, Pallas kernels for 0%

commit v1 on v0

--- a/solution.py
+++ b/solution.py
@@ -75,7 +75,9 @@
     block_tokens = tokens_here * owner_count
     col_index = lax.axis_index("col")
     left_every, mask_every = (
-        lax.all_gather(left_part, "row", axis=2, tiled=True),
+        jnp.concatenate(
+            lax.all_to_all(jnp.stack([left_part] * lax.axis_size("row")), "row", 0, 0), axis=2
+        ),
         lax.all_gather(mask_shaped, "row", axis=2, tiled=True),
     )
     left_block = lax.dynamic_slice_in_dim(left_every, col_index * block_tokens, block_tokens, 2)

time: 390 us -> 493 us (1.26)
  waiting for transfers between devices: 299 us -> 390 us
  local copies, waits for them, and re-layouts: 16.3 us -> 23.8 us
  starting transfers between devices: 0.08 us -> 6.9 us
    all_to_all x0 -> x1, waiting for transfers between devices: none -> 187 us  [body(): lax.all_to_all(jnp.stack([left_part] * lax.axis_size('row')), 'row', 0, 0)]
    all_gather x1 -> x0, waiting for transfers between devices: 93.1 us -> none  [body(): lax.all_gather(left_part, 'row', axis=2, tiled=True)]
    all_to_all x0 -> x1, local copies, waits for them, and re-layouts: none -> 8.25 us  [body(): lax.all_to_all(jnp.stack([left_part] * lax.axis_size('row')), 'row', 0, 0)]
    all_to_all x0 -> x1, starting transfers between devices: none -> 6.86 us  [body(): lax.all_to_all(jnp.stack([left_part] * lax.axis_size('row')), 'row', 0, 0)]
    unnamed x24 -> x23, local copies, waits for them, and re-layouts: 12.8 us -> 9.85 us
  transfers between devices with their start and end apart: 3 -> 3, of which waited for: 3 -> 3; matrix products, arithmetic and copies ran while one was open for 1% -> 0% of each run, Pallas kernels for 0% -> 0%
where the time goes in v1:
time: 493 us
  waiting for transfers between devices  390 us (79%)
  local copies, waits for them, and re-layouts  23.8 us (5%)
  other arithmetic  22.4 us (5%)
  matrix products  18.1 us (4%)
  blocking collectives  16.9 us (3%)
  between operations  14.9 us (3%)
  starting transfers between devices  6.9 us (1%)
    all_to_all x1, waiting for transfers between devices, body(): lax.all_to_all(jnp.stack([left_part] * lax.axis_size('row')), 'row', 0, 0)  187 us
    all_gather x1, waiting for transfers between devices, body(): lax.all_gather(alignment_features, 'col', axis=0, tiled=True)  107 us
    psum x1, waiting for transfers between devices, body(): total_pairs = lax.psum(partial_pairs, 'chan')  95.1 us
    dot_general x1, matrix products, body(): jnp.einsum('sci,sje->ijce', left_block, right_every, preferred_element_ty...  11.1 us
  transfers between devices with their start and end apart: 3, of which 3 were waited for; matrix products, arithmetic and copies ran while one was open for 0% of the time, Pallas kernels for 0%

profile of v1, /device:TPU:1, one launch (start us, length us, event | category | flops | bytes accessed | tf_op | source)
XLA Modules:
  0.0 493.2 jit_solution(15239559342583486077)
XLA Ops:
  6.5 0.0 copy-start
  6.5 0.0 all-gather.4.cloned.1.call-start
  6.5 0.7 all-gather.4.cloned.1.call-update
  7.3 0.7 convert_element_type.49
  7.9 9.8 %all-gather.1 = s32[4,1,512]{2,1,0:T(1,128)S(1)} all-gather(s32[1,1,512]{2,1,0:T(1,128)} %bitcast.40), channel_id=1, replica_groups=mesh['row'=8,'col'=4,'chan'=8] {'col'}, dimensions={0}, use_global_device_ids=true | all-gather | bytes 10240 | tf_op jit(solution)/shard_map/all_gather | solution.py:61
  17.8 0.6 fusion.27
  18.4 0.1 broadcast_multiply_fusion
  18.5 0.0 copy-start.4
  18.5 0.0 copy-start.5
  18.5 107.3 %all-gather.4.cloned.1.call-done = bf16[2048,64,64]{0,2,1:T(8,128)(2,1)} async-done(((bf16[512,64,64]{0,2,1:T(8,128)(2,1)}), bf16[2048,64,64]{0,2,1:T(8,128)(2,1)}) %all-gather.4.cloned.1.call-update) | async-done | bytes 16777232 | tf_op jit(solution)/shard_map/all_gather | solution.py:60
  125.9 0.0 copy-start.1
  125.9 7.3 %convert_reduce_fusion = f32[2048,64]{0,1:T(8,128)S(1)} fusion(bf16[2048,64,64]{0,2,1:T(8,128)(2,1)} %all-gather.4.cloned.1.call-done), kind=kLoop, calls=%fused_computation.1 | loop fusion | flops 16646144 | bytes 17301504 | tf_op jit(solution)/shard_map/reduce_sum | solution.py:9
  133.3 3.3 copy-done.1
  136.5 5.4 %fusion.2 = f32[2048,64]{0,1:T(8,128)S(1)} fusion(bf16[2048,64,64]{0,2,1:T(8,128)(2,1)S(1)} %copy-done.1, f32[2048,64]{0,1:T(8,128)S(1)} %broadcast_multiply_fusion.1), kind=kLoop, calls=%fused_computation.4 | loop fusion | flops 33423360 | bytes 17825792 | tf_op jit(solution)/shard_map/reduce_sum | solution.py:10
  141.9 0.1 add_rsqrt_fusion
  142.0 0.0 copy-done.4
  142.0 0.0 copy-done.5
  142.0 0.0 copy-start.3
  142.0 6.6 %fusion.5 = bf16[2048,64,64]{0,2,1:T(8,128)(2,1)S(1)} fusion(bf16[2048,64,64]{0,2,1:T(8,128)(2,1)S(1)} %copy-done.1, f32[64]{0:T(128)S(1)} %copy-done.4, f32[64]{0:T(128)S(1)} %copy-done.5, f32[2048,64]{0,1:T(8,128)S(1)} %add_rsqrt_fusion, f32[2048,64]{0,1:T(8,128)S(1)} %broadcast_multiply_fusion.1), kind=kLoop, calls=%fused_computation.7 | loop fusion | flops 50331648 | bytes 34603520 | tf_op jit(solution)/shard_map/convert_element_type | solution.py:11
  148.7 0.0 copy-start.2
  148.7 5.7 %copy-done.2 = bf16[2048,64,64]{0,2,1:T(8,128)(2,1)} copy-done((bf16[2048,64,64]{0,2,1:T(8,128)(2,1)}, bf16[2048,64,64]{0,2,1:T(8,128)(2,1)S(1)}, u32[]{:S(2)}) %copy-start.2) | copy-done | bytes 16777240
  154.4 0.0 copy-done.3
  154.4 4.4 fusion.13
  158.8 0.6 copy.17
  159.3 4.3 stack.2
  163.6 0.0 copy-start.7
  163.6 6.9 %all-to-all-start = ((bf16[8,2048,4,64]{1,3,2,0:T(8,128)(2,1)}), bf16[8,2048,4,64]{1,3,2,0:T(8,128)(2,1)}, u32[]{:S(2)}, u32[]{:S(2)}) async-start(bf16[8,2048,4,64]{1,3,2,0:T(8,128)(2,1)} %stack.2), calls=%async_computation | async-start | bytes 16777216 | tf_op jit(solution)/shard_map/all_to_all | solution.py:79
  170.5 0.0 all-reduce.3.cloned.1.call-start
  170.5 187.0 %all-to-all-done = bf16[8,2048,4,64]{1,3,2,0:T(8,128)(2,1)} async-done(((bf16[8,2048,4,64]{1,3,2,0:T(8,128)(2,1)}), bf16[8,2048,4,64]{1,3,2,0:T(8,128)(2,1)}, u32[]{:S(2)}, u32[]{:S(2)}) %all-to-all-start) | async-done | bytes 8388640 | tf_op jit(solution)/shard_map/all_to_all | solution.py:79
  357.6 8.2 %copy.18 = bf16[8,2048,4,64]{1,3,0,2:T(8,128)(2,1)} copy(bf16[8,2048,4,64]{1,3,2,0:T(8,128)(2,1)} %all-to-all-done) | data formatting | bytes 16777216 | tf_op jit(solution)/shard_map/all_to_all | solution.py:79
  365.8 0.0 copy-done.7
  365.8 0.0 copy-start.9
  365.8 0.0 copy-start.8
  365.8 0.0 copy-start.6
  365.8 11.1 %fusion.16 = bf16[64,32,4,128]{3,1,2,0:T(8,128)(2,1)S(1)} fusion(bf16[2048,4,512]{0,2,1:T(8,128)(2,1)} %bitcast.37, s32[]{:T(128)S(6)} %select_n.8, f32[2048,64]{0,1:T(8,128)S(1)} %broadcast_multiply_fusion, bf16[2048,64,64]{0,2,1:T(8,128)(2,1)} %copy-done.2, bf16[64,32]{0,1:T(8,128)(2,1)S(1)} %copy-done.7), kind=kOutput, calls=%fused_computation.18 | convolution fusion | flops 4841275392 | bytes 21499908 | tf_op jit(solution)/shard_map/sci,sje->ijce/dot_general | solution.py:85
  376.9 0.0 copy-done
  376.9 2.7 fusion.21
  379.6 0.0 all-reduce.3.cloned.1.call-update
  380.3 0.0 copy-done.9
  380.3 0.6 dynamic-slice.1
  381.5 0.0 copy-done.8
  381.6 0.2 dynamic-update-slice
  381.8 7.0 %all-reduce = s32[512]{0:T(512)S(1)} all-reduce(s32[512]{0:T(512)S(1)} %dynamic-update-slice), channel_id=2, replica_groups=mesh['row'=8,'col'=4,'chan'=8] {'row'}, use_global_device_ids=true, to_apply=%add | all-reduce | flops 512 | bytes 4096
  388.8 0.1 dynamic-slice_convert_fusion
  388.9 0.1 convert_multiply_fusion
  389.0 0.1 multiply_maximum_fusion
  389.0 95.1 %all-reduce.3.cloned.1.call-done = f32[128,64,128]{2,0,1:T(8,128)} async-done(((f32[128,64,128]{2,0,1:T(8,128)}), f32[128,64,128]{2,0,1:T(8,128)}) %all-reduce.3.cloned.1.call-update) | async-done | bytes 4194320 | tf_op jit(solution)/shard_map/psum | solution.py:95
  484.2 0.0 copy-done.6
  484.2 1.2 divide_convert_fusion
  485.4 0.9 copy.21
  (2 shorter events, 0.0 us)
Async XLA Ops:
  6.5 370.4 %copy-start = (bf16[128,128]{1,0:T(8,128)(2,1)S(1)}, bf16[128,128]{1,0:T(8,128)(2,1)}, u32[]{:S(2)}) copy-start(bf16[128,128]{1,0:T(8,128)(2,1)} %param.16) | copy-start | bytes 98308
  6.5 119.3 %all-gather.4.cloned.1.call-start = ((), (), s32[]{:S(2)}) async-start(), calls=%async_computation.1 | async-start | bytes 20971520 | tf_op jit(solution)/shard_map/all_gather | solution.py:60
  18.5 123.5 %copy-start.4 = (f32[64]{0:T(128)S(1)}, f32[64]{0:T(128)}, u32[]{:S(2)}) copy-start(f32[64]{0:T(128)} %param.13) | copy-start | bytes 772
  18.5 123.5 %copy-start.5 = (f32[64]{0:T(128)S(1)}, f32[64]{0:T(128)}, u32[]{:S(2)}) copy-start(f32[64]{0:T(128)} %param.12) | copy-start | bytes 772
  125.9 10.7 %copy-start.1 = (bf16[2048,64,64]{0,2,1:T(8,128)(2,1)S(1)}, bf16[2048,64,64]{0,2,1:T(8,128)(2,1)}, u32[]{:S(2)}) copy-start(bf16[2048,64,64]{0,2,1:T(8,128)(2,1)} %all-gather.4.cloned.1.call-done) | copy-start | bytes 50331652
  142.0 12.4 %copy-start.3 = (bf16[64,4]{0,1:T(4,128)(2,1)S(1)}, bf16[64,4]{0,1:T(4,128)(2,1)}, u32[]{:S(2)}) copy-start(bf16[64,4]{0,1:T(4,128)(2,1)} %param.14) | copy-start | bytes 1540
  148.7 5.7 %copy-start.2 = (bf16[2048,64,64]{0,2,1:T(8,128)(2,1)}, bf16[2048,64,64]{0,2,1:T(8,128)(2,1)S(1)}, u32[]{:S(2)}) copy-start(bf16[2048,64,64]{0,2,1:T(8,128)(2,1)S(1)} %fusion.5) | copy-start | bytes 50331652
  163.6 202.2 %copy-start.7 = (bf16[64,32]{0,1:T(8,128)(2,1)S(1)}, bf16[64,32]{0,1:T(8,128)(2,1)}, u32[]{:S(2)}) copy-start(bf16[64,32]{0,1:T(8,128)(2,1)} %param.15) | copy-start | bytes 12292
  163.6 193.9 %all-to-all-start = ((bf16[8,2048,4,64]{1,3,2,0:T(8,128)(2,1)}), bf16[8,2048,4,64]{1,3,2,0:T(8,128)(2,1)}, u32[]{:S(2)}, u32[]{:S(2)}) async-start(bf16[8,2048,4,64]{1,3,2,0:T(8,128)(2,1)} %stack.2), calls=%async_computation | async-start | bytes 16777216 | tf_op jit(solution)/shard_map/all_to_all | solution.py:79
  170.5 313.7 %all-reduce.3.cloned.1.call-start = ((), (), s32[]{:S(2)}) async-start(), calls=%async_computation.2 | async-start | bytes 8388608 | tf_op jit(solution)/shard_map/psum | solution.py:95
  365.8 14.5 %copy-start.9 = (u32[256]{0:T(256)S(1)}, u32[256]{0:T(256)}, u32[]{:S(2)}) copy-start(u32[256]{0:T(256)} %constant.32) | copy-start | bytes 3076
  365.8 15.7 %copy-start.8 = (s32[64]{0:T(128)S(1)}, s32[64]{0:T(128)}, u32[]{:S(2)}) copy-start(s32[64]{0:T(128)} %param.11) | copy-start | bytes 772
  365.8 118.4 %copy-start.6 = (f32[128]{0:T(128)S(1)}, f32[128]{0:T(128)}, u32[]{:S(2)}) copy-start(f32[128]{0:T(128)} %param.17) | copy-start | bytes 1540
Sparse Core Ops, SparseCore 0:
  9.1 116.6 all-gather.3
  379.8 104.3 all-reduce.2
